TPU v7x, 256 devices: a whole 4x4x8 slice. The times are simulated.
256 devices in a mesh: gx: 4 (over x_lo, core), gy: 8 (over z), gz: 8 (over x_hi, y).
Axes of the slice: x: 4 (x_hi: 2, x_lo: 2; x = x_hi * 2 + x_lo), y: 4, z: 8, core: 2. Of those that a mesh axis runs over, the one named last changes fastest.
Arguments:
- traces: bfloat16 [2, 4, 8, 8, 512, 768], P(None, 'gx', 'gy', 'gz'), may hold values from -6 to 6
- sources: bfloat16 [2, 4, 8, 8, 512, 768], P(None, 'gx', 'gy', 'gz'), may hold values from -4 to 4
- local_ops: bfloat16 [2, 4, 8, 8, 768, 768], P(None, 'gx', 'gy', 'gz'), may hold values from -0.15625 to 0.15625
- plane_coupling: bfloat16 [4, 64, 64], P('gx'), may hold values from -0.375 to 0.375
- face_owner: int32 [4, 64], P('gx'), may hold values from 0 to 63, each once within a row
Outputs:
- new_traces: bfloat16 [2, 4, 8, 8, 512, 768], P(None, 'gx', 'gy', 'gz')
Inputs may be any that keep to these rules, and one draw needn't show every extreme that they name: `face_owner`: each row is a permutation of the 64 plane positions.
All inputs are finite; a program needn't handle non-finite values.
Results may differ from a plain program's by a relative error of at most 0.0062.
Values may be sent and summed in bfloat16 or wider, within the bound.
A program may use at most 64 MiB of HBM per device.

v0:
```python
import jax
import jax.numpy as jnp
from jax import lax
from jax.sharding import PartitionSpec as P

SWEEPS = 2


def with_halo(block, sides, width):
    for axis, dim in sides:
        count = lax.axis_size(axis)
        forward = [(i, i + 1) for i in range(count - 1)]
        forward.append((count - 1, 0))
        backward = [(target, source) for source, target in forward]
        low = lax.ppermute(
            lax.slice_in_dim(block, block.shape[dim] - width, None, axis=dim), axis, forward
        )
        high = lax.ppermute(lax.slice_in_dim(block, 0, width, axis=dim), axis, backward)
        block = jnp.concatenate([low, block, high], axis=dim)
    return block


def on_device(traces, sources, local_ops, plane_coupling, face_owner):
    columns_all = local_ops.shape[-1]
    slab_width = columns_all // 6
    slab_rows = traces.shape[4]
    count_y = lax.axis_size("gy")
    count_z = lax.axis_size("gz")
    plane_size = count_y * count_z
    block_rows_count = slab_rows // plane_size
    operators = local_ops.reshape(2, columns_all, columns_all)
    source_rows = sources.reshape(2, slab_rows, columns_all).astype(jnp.float32)
    incoming = traces.reshape(2, slab_rows, columns_all)
    owners = face_owner.reshape(plane_size)
    select = (owners[:, None] == jnp.arange(plane_size, dtype=jnp.int32)[None, :]).astype(
        jnp.float32
    )
    mixing = jnp.dot(
        plane_coupling.reshape(plane_size, plane_size).astype(jnp.float32),
        select,
        precision=lax.Precision.HIGHEST,
    ).astype(jnp.bfloat16)
    for sweep_step in range(SWEEPS):
        real_part = (
            jnp.dot(incoming[0], operators[0], preferred_element_type=jnp.float32)
            - jnp.dot(incoming[1], operators[1], preferred_element_type=jnp.float32)
            + source_rows[0]
        )
        imag_part = (
            jnp.dot(incoming[0], operators[1], preferred_element_type=jnp.float32)
            + jnp.dot(incoming[1], operators[0], preferred_element_type=jnp.float32)
            + source_rows[1]
        )
        outgoing = (
            jnp.stack([real_part, imag_part])
            .astype(jnp.bfloat16)
            .reshape(2, slab_rows, 6, slab_width)
        )
        along_x = with_halo(outgoing[:, :, 0:2, :], (("gx", 2),), 1)
        partial_faces = jnp.concatenate(
            [along_x[:, :, 0:1], along_x[:, :, 3:4], outgoing[:, :, 2:6]], axis=2
        )
        blocks = partial_faces.reshape(2, plane_size, block_rows_count, 6, slab_width)
        update_block_rows = lax.all_to_all(
            blocks, ("gy", "gz"), split_axis=1, concat_axis=1, tiled=True
        )
        row_count = update_block_rows.shape[2]
        grid_view = update_block_rows.reshape(2, count_y, count_z, row_count, 6, slab_width)
        moved = jnp.stack(
            [
                grid_view[:, :, :, :, 0],
                grid_view[:, :, :, :, 1],
                jnp.roll(grid_view[:, :, :, :, 3], 1, axis=1),
                jnp.roll(grid_view[:, :, :, :, 2], -1, axis=1),
                jnp.roll(grid_view[:, :, :, :, 5], 1, axis=2),
                jnp.roll(grid_view[:, :, :, :, 4], -1, axis=2),
            ],
            axis=4,
        )
        block_rows = moved.reshape(2, plane_size, row_count * columns_all)
        coupled = jnp.einsum("pq,rqc->rpc", mixing, block_rows, preferred_element_type=jnp.float32)
        updated = (block_rows.astype(jnp.float32) - coupled).astype(jnp.bfloat16)
        updated = updated.reshape(2, plane_size, row_count, 6, slab_width)
        returned = lax.all_to_all(updated, ("gy", "gz"), split_axis=1, concat_axis=1, tiled=True)
        incoming = returned.reshape(2, slab_rows, columns_all)
    return incoming.reshape(traces.shape)


def solution(mesh):
    placed = (
        P(None, "gx", "gy", "gz", None, None),
        P(None, "gx", "gy", "gz", None, None),
        P(None, "gx", "gy", "gz", None, None),
        P("gx", None, None),
        P("gx", None),
    )
    return jax.shard_map(
        on_device,
        mesh=mesh,
        in_specs=placed,
        out_specs=P(None, "gx", "gy", "gz", None, None),
        check_vma=False,
    )
```

profile of v0, /device:TPU:34, one launch (start us, length us, event | category | flops | bytes accessed | tf_op | source)
XLA Modules:
  0.0 266.4 jit_solution(3088411182501243371)
XLA Ops:
  0.0 0.0 copy-start
  0.0 2.4 fusion.15
  2.5 0.0 copy-start.8
  2.5 2.0 fusion.22
  4.5 0.0 copy-done.8
  4.5 0.0 copy-start.9
  4.5 0.2 convert_element_type.26
  4.8 1.2 copy-done.9
  5.9 1.7 add_convert_fusion.2
  7.6 1.7 add_convert_fusion.3
  9.4 2.3 copy.56
  11.7 2.3 copy.57
  14.0 1.3 pad_maximum_fusion.3
  15.3 0.1 collective-permute-start
  15.3 1.7 collective-permute-start.1
  17.1 6.0 %collective-permute-done = bf16[2,512,1,128]{1,3,2,0:T(8,128)(2,1)S(1)} collective-permute-done((bf16[2,512,1,128]{1,3,2,0:T(8,128)(2,1)S(1)}, bf16[2,512,1,128]{1,3,2,0:T(8,128)(2,1)S(1)}, u32[]{:S(2)}, u32[]{:S(2)}) %collective-permute-start) | collective-permute-done | bytes 262176 | tf_op jit(solution)/shard_map/ppermute | solution.py:15
  23.1 0.0 collective-permute-done.1
  23.1 0.0 copy-done.6
  23.1 1.3 fusion.9
  24.4 2.6 copy.58
  27.1 2.8 %copy.59 = bf16[2,64,8,6,128]{4,2,3,0,1:T(8,128)(2,1)} copy(bf16[2,64,8,6,128]{4,2,1,3,0:T(8,128)(2,1)} %bitcast.168) | data formatting | bytes 3145728 | tf_op jit(solution)/shard_map/reshape | solution.py:63
  29.9 13.3 %all-to-all-start = ((bf16[2,64,8,6,128]{4,2,3,0,1:T(8,128)(2,1)}), bf16[2,64,8,6,128]{4,2,3,0,1:T(8,128)(2,1)}, u32[]{:S(2)}, u32[]{:S(2)}) async-start(bf16[2,64,8,6,128]{4,2,3,0,1:T(8,128)(2,1)} %copy.59), calls=%async_computation | async-start | bytes 3145728 | tf_op jit(solution)/shard_map/all_to_all | solution.py:64
  43.2 0.2 fusion.24
  43.5 40.4 %all-to-all-done = bf16[2,64,8,6,128]{4,2,3,0,1:T(8,128)(2,1)} async-done(((bf16[2,64,8,6,128]{4,2,3,0,1:T(8,128)(2,1)}), bf16[2,64,8,6,128]{4,2,3,0,1:T(8,128)(2,1)}, u32[]{:S(2)}, u32[]{:S(2)}) %all-to-all-start) | async-done | bytes 1572896 | tf_op jit(solution)/shard_map/all_to_all | solution.py:64
  83.8 1.5 copy.60
  85.3 0.3 slice_bitcast_fusion.12
  85.9 0.1 fusion.41
  85.9 0.1 fusion.42
  86.0 0.1 fusion.43
  86.1 0.1 fusion.44
  86.2 0.4 copy.65
  86.6 1.8 fusion.3
  88.3 4.5 %reshape.67 = bf16[2,64,8,6,128]{4,3,2,1,0:T(8,128)(2,1)} reshape(bf16[2,64,6144]{2,1,0:T(8,128)(2,1)} %fusion.3) | data formatting | bytes 3145728 | tf_op jit(solution)/shard_map/reshape | solution.py:83
  92.9 1.9 copy.67
  94.8 0.0 copy-start.2
  94.8 47.1 %all_to_all.20 = bf16[2,64,8,6,128]{4,2,3,0,1:T(8,128)(2,1)S(1)} all-to-all(bf16[2,64,8,6,128]{4,2,3,0,1:T(8,128)(2,1)S(1)} %copy.67), channel_id=1, replica_groups=mesh['gx'=4,'gy'=8,'gz'=8] {'gy','gz'}, dimensions={1} | all-to-all | bytes 3145728 | tf_op jit(solution)/shard_map/all_to_all | solution.py:84
  141.9 0.8 fusion.12
  142.7 0.4 copy-done.7
  143.0 1.7 add_convert_fusion
  144.8 2.3 copy.71
  147.1 2.4 fusion.19
  149.5 0.0 copy-done.3
  149.5 2.9 %add_convert_fusion.1 = bf16[512,768]{1,0:T(8,128)(2,1)} fusion(f32[512,768]{1,0:T(8,128)S(1)} %fusion.19, f32[2,1,1,1,512,768]{5,4,3,2,1,0:T(8,128)S(1)} %convert_element_type.26, bf16[2,1,1,1,768,768]{5,4,3,2,1,0:T(8,128)(2,1)S(1)} %copy-done.3, bf16[2,64,8,6,128]{4,2,3,0,1:T(8,128)(2,1)} %copy-done.7), kind=kOutput, calls=%fused_computation.19 | convolution fusion | flops 605159424 | bytes 5898240 | tf_op jit(solution)/shard_map/dot_general | solution.py:46
  152.4 1.5 copy.70
  154.0 0.1 collective-permute-start.2
  154.1 1.7 collective-permute-start.3
  155.8 5.1 %collective-permute-done.2 = bf16[2,512,1,128]{1,3,2,0:T(8,128)(2,1)S(1)} collective-permute-done((bf16[2,512,1,128]{1,3,2,0:T(8,128)(2,1)S(1)}, bf16[2,512,1,128]{1,3,2,0:T(8,128)(2,1)S(1)}, u32[]{:S(2)}, u32[]{:S(2)}) %collective-permute-start.2) | collective-permute-done | bytes 262176 | tf_op jit(solution)/shard_map/ppermute | solution.py:15
  160.9 0.7 collective-permute-done.3
  161.6 0.1 fusion.11
  161.7 0.9 copy.72
  162.7 0.3 copy.73
  162.9 48.3 %all_to_all.21 = bf16[2,64,8,6,128]{4,2,3,0,1:T(8,128)(2,1)S(1)} all-to-all(bf16[2,64,8,6,128]{4,2,3,0,1:T(8,128)(2,1)S(1)} %copy.73), channel_id=1, replica_groups=mesh['gx'=4,'gy'=8,'gz'=8] {'gy','gz'}, dimensions={1} | all-to-all | bytes 3145728 | tf_op jit(solution)/shard_map/all_to_all | solution.py:64
  211.2 0.1 copy.74
  211.3 0.3 slice_bitcast_fusion.8
  211.8 0.1 fusion.45
  211.9 0.1 fusion.46
  212.0 0.1 fusion.47
  212.1 0.1 fusion.48
  212.2 0.4 copy.79
  212.6 1.8 fusion.2
  214.3 3.6 %reshape.71 = bf16[2,64,8,6,128]{4,3,2,1,0:T(8,128)(2,1)S(1)} reshape(bf16[2,64,6144]{2,1,0:T(8,128)(2,1)} %fusion.2) | data formatting | bytes 3145728 | tf_op jit(solution)/shard_map/reshape | solution.py:83
  217.9 0.3 copy.81
  218.2 47.0 %all_to_all.22 = bf16[2,64,8,6,128]{4,2,3,0,1:T(8,128)(2,1)S(1)} all-to-all(bf16[2,64,8,6,128]{4,2,3,0,1:T(8,128)(2,1)S(1)} %copy.81), channel_id=1, replica_groups=mesh['gx'=4,'gy'=8,'gz'=8] {'gy','gz'}, dimensions={1} | all-to-all | bytes 3145728 | tf_op jit(solution)/shard_map/all_to_all | solution.py:84
  265.2 1.2 copy.91
  (32 shorter events, 0.4 us)
Async XLA Ops:
  0.0 43.2 %copy-start = (bf16[1,64,64]{2,1,0:T(8,128)(2,1)S(1)}, bf16[1,64,64]{2,1,0:T(8,128)(2,1)}, u32[]{:S(2)}) copy-start(bf16[1,64,64]{2,1,0:T(8,128)(2,1)} %param.8) | copy-start | bytes 24580
  0.0 2.4 copy-start.1
  2.5 2.0 copy-start.8
  4.5 1.4 copy-start.9
  14.0 9.1 %copy-start.5 = (bf16[512,768]{0,1:T(8,128)(2,1)S(1)}, bf16[512,768]{0,1:T(8,128)(2,1)}, u32[]{:S(2)}) copy-start(bf16[512,768]{0,1:T(8,128)(2,1)} %copy.56) | copy-start | bytes 2359300
  14.0 9.1 %copy-start.6 = (bf16[512,768]{0,1:T(8,128)(2,1)S(1)}, bf16[512,768]{0,1:T(8,128)(2,1)}, u32[]{:S(2)}) copy-start(bf16[512,768]{0,1:T(8,128)(2,1)} %copy.57) | copy-start | bytes 2359300
  15.3 7.8 %collective-permute-start = (bf16[2,512,1,128]{1,3,2,0:T(8,128)(2,1)S(1)}, bf16[2,512,1,128]{1,3,2,0:T(8,128)(2,1)S(1)}, u32[]{:S(2)}, u32[]{:S(2)}) collective-permute-start(bf16[2,512,1,128]{1,3,2,0:T(8,128)(2,1)S(1)} %get-tuple-element.15), channel_id=1, source_target_pairs={{0,64},{64,128},{128,192},{192,0},{1,65},{65,129},{129,193},{193,1... | collective-permute-start | bytes 786440 | tf_op jit(solution)/shard_map/ppermute | solution.py:15
  15.3 7.8 %collective-permute-start.1 = (bf16[2,512,1,128]{1,3,2,0:T(8,128)(2,1)S(1)}, bf16[2,512,1,128]{1,3,2,0:T(8,128)(2,1)S(1)}, u32[]{:S(2)}, u32[]{:S(2)}) collective-permute-start(bf16[2,512,1,128]{1,3,2,0:T(8,128)(2,1)S(1)} %get-tuple-element.16), channel_id=1, source_target_pairs={{64,0},{128,64},{192,128},{0,192},{65,1},{129,65},{193,129},{1,193... | collective-permute-start | bytes 786440 | tf_op jit(solution)/shard_map/ppermute | solution.py:18
  29.9 13.3 %copy-start.10 = (s32[1,64]{1,0:T(1,128)S(1)}, s32[1,64]{1,0:T(1,128)}, u32[]{:S(2)}) copy-start(s32[1,64]{1,0:T(1,128)} %param.9) | copy-start | bytes 772
  29.9 54.0 %all-to-all-start = ((bf16[2,64,8,6,128]{4,2,3,0,1:T(8,128)(2,1)}), bf16[2,64,8,6,128]{4,2,3,0,1:T(8,128)(2,1)}, u32[]{:S(2)}, u32[]{:S(2)}) async-start(bf16[2,64,8,6,128]{4,2,3,0,1:T(8,128)(2,1)} %copy.59), calls=%async_computation | async-start | bytes 3145728 | tf_op jit(solution)/shard_map/all_to_all | solution.py:64
  94.8 47.1 %copy-start.2 = (bf16[2,1,1,1,768,768]{5,4,3,2,1,0:T(8,128)(2,1)S(1)}, bf16[2,1,1,1,768,768]{5,4,3,2,1,0:T(8,128)(2,1)}, u32[]{:S(2)}) copy-start(bf16[2,1,1,1,768,768]{5,4,3,2,1,0:T(8,128)(2,1)} %param.7) | copy-start | bytes 7077892
  141.9 1.1 copy-start.7
  147.1 2.4 copy-start.3
  152.4 1.5 copy-start.4
  154.0 7.0 %collective-permute-start.2 = (bf16[2,512,1,128]{1,3,2,0:T(8,128)(2,1)S(1)}, bf16[2,512,1,128]{1,3,2,0:T(8,128)(2,1)S(1)}, u32[]{:S(2)}, u32[]{:S(2)}) collective-permute-start(bf16[2,512,1,128]{1,3,2,0:T(8,128)(2,1)S(1)} %get-tuple-element.9), channel_id=1, source_target_pairs={{0,64},{64,128},{128,192},{192,0},{1,65},{65,129},{129,193},{193,1... | collective-permute-start | bytes 786440 | tf_op jit(solution)/shard_map/ppermute | solution.py:15
  154.1 7.5 %collective-permute-start.3 = (bf16[2,512,1,128]{1,3,2,0:T(8,128)(2,1)S(1)}, bf16[2,512,1,128]{1,3,2,0:T(8,128)(2,1)S(1)}, u32[]{:S(2)}, u32[]{:S(2)}) collective-permute-start(bf16[2,512,1,128]{1,3,2,0:T(8,128)(2,1)S(1)} %get-tuple-element.10), channel_id=1, source_target_pairs={{64,0},{128,64},{192,128},{0,192},{65,1},{129,65},{193,129},{1,193... | collective-permute-start | bytes 786440 | tf_op jit(solution)/shard_map/ppermute | solution.py:18
where the time goes:
time: 269 us; the launch traced here: 266 us
  blocking collectives  142 us (53%)
  waiting for transfers between devices  52.2 us (19%)
  local copies, waits for them, and re-layouts  31.3 us (12%)
  matrix products  19.5 us (7%)
  starting transfers between devices  17 us (6%)
  other arithmetic  3.57 us (1%)
    all_to_all x2, blocking collectives, on_device(): lax.all_to_all(updated, ('gy', 'gz'), split_axis=1, concat_axis=1, tiled=...  94.1 us
    all_to_all x1, blocking collectives, on_device(): lax.all_to_all(blocks, ('gy', 'gz'), split_axis=1, concat_axis=1, tiled=T...  48.3 us
    all_to_all x1, waiting for transfers between devices, on_device(): lax.all_to_all(blocks, ('gy', 'gz'), split_axis=1, concat_axis=1, tiled=T...  40.4 us
    all_to_all x1, starting transfers between devices, on_device(): lax.all_to_all(blocks, ('gy', 'gz'), split_axis=1, concat_axis=1, tiled=T...  13.3 us
    ppermute x2, waiting for transfers between devices, with_halo(): lax.ppermute(lax.slice_in_dim(block, block.shape[dim] - width, None, axis...  11.2 us
    reshape x4, local copies, waits for them, and re-layouts, on_device(): updated = updated.reshape(2, plane_size, row_count, 6, slab_width)  10.2 us
    another operation x4, local copies, waits for them, and re-layouts  8.4 us
  transfers between devices with their start and end apart: 5, of which 4 were waited for; matrix products, arithmetic and copies ran while one was open for 0% of the time, Pallas kernels for 0%

commit v1 on v0

v1 whole, which is shorter than its diff:
```python
import functools

import jax
import jax.numpy as jnp
from jax import lax
from jax.experimental import pallas as pl
from jax.experimental.pallas import tpu as pltpu
from jax.sharding import PartitionSpec as P

SWEEPS = 2
FACES = 6
W = 128
SUB = 16
ORDER = (3, 2, 5, 4, 0, 1)
SHIFT_Y = {2: 1, 3: -1}
SHIFT_Z = {4: 1, 5: -1}
MESH = pl.DeviceIdType.MESH


def kernel(
    nx, ny, nz, slabs,
    traces, sources, ops, coupling, owners, out,
    in0, in1, in2, sent, xr, zr, kr, ur, zs, sv, bv, mi,
    load_sem, out_sem, xs_sem, xr_sem, s_sem, r_sem,
):
    i = lax.axis_index("gx")
    j = lax.axis_index("gy")
    k = lax.axis_index("gz")
    rows = 2 * slabs
    block = rows // ny
    plane = ny * nz
    incoming = (in0, in1, in2)

    for c in range(2):
        for f in range(FACES):
            pltpu.make_async_copy(
                traces.at[c, :, pl.ds(f * W, W)],
                in0.at[f, pl.ds(c * slabs, slabs), :],
                load_sem.at[0],
            ).start()
    load_ops = pltpu.make_async_copy(ops, sv, load_sem.at[1])
    load_ops.start()
    load_sources = pltpu.make_async_copy(sources, bv, load_sem.at[2])
    load_sources.start()

    barrier = pltpu.get_barrier_semaphore()
    left = lax.rem(i + nx - 1, nx)
    right = lax.rem(i + 1, nx)
    for target in (left, right):
        pl.semaphore_signal(barrier, inc=1, device_id={"gx": target}, device_id_type=MESH)
    for d in range(1, ny):
        pl.semaphore_signal(
            barrier, inc=1, device_id={"gy": lax.rem(j + d, ny)}, device_id_type=MESH
        )
    for d in range(1, nz):
        pl.semaphore_signal(
            barrier, inc=1, device_id={"gz": lax.rem(k + d, nz)}, device_id_type=MESH
        )

    def local_solve(s, f):
        w = jnp.concatenate([sv[0, :, f * W:(f + 1) * W], sv[1, :, f * W:(f + 1) * W]], axis=1)
        step = min(256, slabs)
        source = incoming[s]

        def part(t, carry):
            at = pl.multiple_of(t * step, step)
            im_at = pl.multiple_of(slabs + t * step, step)
            re = jnp.concatenate([source[g, pl.ds(at, step), :] for g in range(FACES)], axis=1)
            im = jnp.concatenate([source[g, pl.ds(im_at, step), :] for g in range(FACES)], axis=1)
            p = jnp.dot(re, w, preferred_element_type=jnp.float32)
            q = jnp.dot(im, w, preferred_element_type=jnp.float32)
            b0 = bv[0, pl.ds(at, step), f * W:(f + 1) * W].astype(jnp.float32)
            b1 = bv[1, pl.ds(at, step), f * W:(f + 1) * W].astype(jnp.float32)
            sent[s, f, pl.ds(at, step), :] = (p[:, :W] - q[:, W:] + b0).astype(jnp.bfloat16)
            sent[s, f, pl.ds(im_at, step), :] = (p[:, W:] + q[:, :W] + b1).astype(jnp.bfloat16)
            return carry

        lax.fori_loop(0, slabs // step, part, 0)

    def ring(n, body):
        def step(t, carry):
            half = (t + 1) // 2
            odd = lax.rem(t, 2)
            body(odd * half + (1 - odd) * (n - half))
            return carry

        lax.fori_loop(1, n, step, 0)

    def z_send(s, g, face):
        slot = lax.rem(j + SHIFT_Y.get(g, 0) + ny, ny)

        def one(d):
            to = lax.rem(j + d, ny)
            pltpu.make_async_remote_copy(
                src_ref=face.at[pl.ds(pl.multiple_of(to * block, block), block), :],
                dst_ref=zr.at[s, g, slot],
                send_sem=s_sem.at[s, 0, g],
                recv_sem=r_sem.at[s, 0, g],
                device_id={"gy": to},
                device_id_type=MESH,
            ).start()

        ring(ny, one)
        pltpu.make_async_copy(
            face.at[pl.ds(pl.multiple_of(j * block, block), block), :],
            zr.at[s, g, slot],
            r_sem.at[s, 0, g],
        ).start()

    def k_send(s, g):
        slot = lax.rem(k + SHIFT_Z.get(g, 0) + nz, nz)

        def one(d):
            to = lax.rem(k + d, nz)
            pltpu.make_async_remote_copy(
                src_ref=zr.at[s, g, :, pl.ds(pl.multiple_of(to * SUB, SUB), SUB), :],
                dst_ref=kr.at[s, g, slot],
                send_sem=s_sem.at[s, 1, g],
                recv_sem=r_sem.at[s, 1, g],
                device_id={"gz": to},
                device_id_type=MESH,
            ).start()

        ring(nz, one)
        pltpu.make_async_copy(
            zr.at[s, g, :, pl.ds(pl.multiple_of(k * SUB, SUB), SUB), :],
            kr.at[s, g, slot],
            r_sem.at[s, 1, g],
        ).start()

    def update(s, g):
        step = min(256, rows)
        values = kr[s, g].reshape(rows, W)

        def part(t, carry):
            at = pl.multiple_of(t * step, step)
            slots = step // (ny * SUB)
            first = t * slots
            coupled = jnp.dot(mi[pl.ds(at, step), :], values, preferred_element_type=jnp.float32)
            mine = kr[s, g, pl.ds(first, slots)].reshape(step, W).astype(jnp.float32)
            ur[s, g, pl.ds(first, slots)] = (
                (mine - coupled).astype(jnp.bfloat16).reshape(slots, ny, SUB, W)
            )
            return carry

        lax.fori_loop(0, rows // step, part, 0)

    def k_return(s, g):
        mine = pl.ds(pl.multiple_of(k * SUB, SUB), SUB)

        def one(d):
            to = lax.rem(k + d, nz)
            pltpu.make_async_remote_copy(
                src_ref=ur.at[s, g, to],
                dst_ref=zs.at[s, g, :, mine, :],
                send_sem=s_sem.at[s, 2, g],
                recv_sem=r_sem.at[s, 2, g],
                device_id={"gz": to},
                device_id_type=MESH,
            ).start()

        ring(nz, one)
        pltpu.make_async_copy(
            ur.at[s, g, k], zs.at[s, g, :, mine, :], r_sem.at[s, 2, g]
        ).start()

    def z_return(s, g):
        mine = pl.ds(pl.multiple_of(j * block, block), block)
        target = incoming[s + 1]

        def one(d):
            to = lax.rem(j + d, ny)
            pltpu.make_async_remote_copy(
                src_ref=zs.at[s, g, to],
                dst_ref=target.at[g, mine, :],
                send_sem=s_sem.at[s, 3, g],
                recv_sem=r_sem.at[s, 3, g],
                device_id={"gy": to},
                device_id_type=MESH,
            ).start()

        ring(ny, one)
        pltpu.make_async_copy(
            zs.at[s, g, j], target.at[g, mine, :], r_sem.at[s, 3, g]
        ).start()

    def arrive(sem, ref):
        pltpu.make_async_copy(ref, ref, sem).wait()

    def x_send(s, f, to, slot):
        pltpu.make_async_remote_copy(
            src_ref=sent.at[s, f],
            dst_ref=xr.at[s, slot],
            send_sem=xs_sem.at[s, slot],
            recv_sem=xr_sem.at[s, slot],
            device_id={"gx": to},
            device_id_type=MESH,
        ).start()

    def build_mixing():
        owner = jnp.broadcast_to(owners[...], (plane, plane))
        pick = (owner == lax.broadcasted_iota(jnp.int32, (plane, plane), 1)).astype(jnp.bfloat16)
        mixing = jnp.dot(coupling[...], pick, preferred_element_type=jnp.float32)
        mixing = mixing.astype(jnp.bfloat16)

        def place(index):
            point = index // SUB
            return lax.rem(point, ny) * nz + point // ny

        column = lax.broadcasted_iota(jnp.int32, (plane, rows), 1)
        spread = (lax.broadcasted_iota(jnp.int32, (plane, rows), 0) == place(column)).astype(
            jnp.bfloat16
        )
        right_part = jnp.dot(mixing, spread, preferred_element_type=jnp.float32).astype(
            jnp.bfloat16
        )
        step = min(128, rows)

        def part(t, carry):
            at = pl.multiple_of(t * step, step)
            row = lax.broadcasted_iota(jnp.int32, (step, plane), 0) + at
            choose = (place(row) == lax.broadcasted_iota(jnp.int32, (step, plane), 1)).astype(
                jnp.bfloat16
            )
            full = jnp.dot(choose, right_part, preferred_element_type=jnp.float32)
            same = lax.rem(
                lax.broadcasted_iota(jnp.int32, (step, rows), 0), SUB
            ) == lax.rem(lax.broadcasted_iota(jnp.int32, (step, rows), 1), SUB)
            mi[pl.ds(at, step), :] = jnp.where(same, full, 0.0).astype(jnp.bfloat16)
            return carry

        lax.fori_loop(0, rows // step, part, 0)

    arrive(load_sem.at[0], in0)
    load_ops.wait()
    load_sources.wait()
    pl.semaphore_wait(barrier, 2 + (ny - 1) + (nz - 1))

    for s in range(SWEEPS):
        local_solve(s, 2)
        z_send(s, 3, sent.at[s, 2])
        local_solve(s, 0)
        x_send(s, 0, left, 1)
        local_solve(s, 1)
        x_send(s, 1, right, 0)
        for g in ORDER[1:4]:
            local_solve(s, g ^ 1)
            z_send(s, g, sent.at[s, g ^ 1])
        if s == 0:
            build_mixing()
        for g in ORDER[4:]:
            arrive(xr_sem.at[s, g], xr.at[s, g])
            z_send(s, g, xr.at[s, g])
        for t in range(FACES + 2):
            if t < FACES:
                g = ORDER[t]
                arrive(r_sem.at[s, 0, g], zr.at[s, g])
                k_send(s, g)
            if 1 <= t <= FACES:
                g = ORDER[t - 1]
                arrive(r_sem.at[s, 1, g], kr.at[s, g])
                update(s, g)
                k_return(s, g)
            if t >= 2:
                g = ORDER[t - 2]
                arrive(r_sem.at[s, 2, g], zs.at[s, g])
                z_return(s, g)
        target = incoming[s + 1]
        for g in ORDER:
            arrive(r_sem.at[s, 3, g], target.at[g])
            if s == SWEEPS - 1:
                for c in range(2):
                    pltpu.make_async_copy(
                        target.at[g, pl.ds(c * slabs, slabs), :],
                        out.at[c, :, pl.ds(g * W, W)],
                        out_sem.at[g],
                    ).start()

    for s in range(SWEEPS):
        for g in range(FACES):
            arrive(s_sem.at[s, 0, g], zr.at[s, g, pl.ds(0, ny - 1)])
            arrive(s_sem.at[s, 1, g], kr.at[s, g, pl.ds(0, nz - 1)])
            arrive(s_sem.at[s, 2, g], kr.at[s, g, pl.ds(0, nz - 1)])
            arrive(s_sem.at[s, 3, g], zr.at[s, g, pl.ds(0, ny - 1)])
        for slot in range(2):
            arrive(xs_sem.at[s, slot], xr.at[s, slot])
    for g in range(FACES):
        arrive(out_sem.at[g], in2.at[g])


def on_device(nx, ny, nz, traces, sources, local_ops, plane_coupling, face_owner):
    slabs = traces.shape[4]
    columns = traces.shape[5]
    rows = 2 * slabs
    plane = ny * nz
    block = rows // ny
    bf16 = jnp.bfloat16
    hbm = pl.BlockSpec(memory_space=pl.ANY)
    vmem = pl.BlockSpec(memory_space=pltpu.VMEM)
    faces = (FACES, rows, W)
    out = pl.pallas_call(
        functools.partial(kernel, nx, ny, nz, slabs),
        out_shape=jax.ShapeDtypeStruct((2, slabs, columns), bf16),
        in_specs=[hbm, hbm, hbm, vmem, vmem],
        out_specs=hbm,
        scratch_shapes=[
            pltpu.VMEM(faces, bf16),
            pltpu.VMEM(faces, bf16),
            pltpu.VMEM(faces, bf16),
            pltpu.VMEM((SWEEPS,) + faces, bf16),
            pltpu.VMEM((SWEEPS, 2, rows, W), bf16),
            pltpu.VMEM((SWEEPS, FACES, ny, block, W), bf16),
            pltpu.VMEM((SWEEPS, FACES, nz, ny, SUB, W), bf16),
            pltpu.VMEM((SWEEPS, FACES, nz, ny, SUB, W), bf16),
            pltpu.VMEM((SWEEPS, FACES, ny, block, W), bf16),
            pltpu.VMEM((2, columns, columns), bf16),
            pltpu.VMEM((2, slabs, columns), bf16),
            pltpu.VMEM((rows, rows), bf16),
            pltpu.SemaphoreType.DMA((3,)),
            pltpu.SemaphoreType.DMA((FACES,)),
            pltpu.SemaphoreType.DMA((SWEEPS, 2)),
            pltpu.SemaphoreType.DMA((SWEEPS, 2)),
            pltpu.SemaphoreType.DMA((SWEEPS, 4, FACES)),
            pltpu.SemaphoreType.DMA((SWEEPS, 4, FACES)),
        ],
        compiler_params=pltpu.CompilerParams(
            collective_id=0, has_side_effects=True, vmem_limit_bytes=60 << 20
        ),
    )(
        traces.reshape(2, slabs, columns),
        sources.reshape(2, slabs, columns),
        local_ops.reshape(2, columns, columns),
        plane_coupling.reshape(plane, plane),
        face_owner.reshape(plane, 1),
    )
    return out.reshape(traces.shape)


def solution(mesh):
    placed = (
        P(None, "gx", "gy", "gz", None, None),
        P(None, "gx", "gy", "gz", None, None),
        P(None, "gx", "gy", "gz", None, None),
        P("gx", None, None),
        P("gx", None),
    )
    sizes = tuple(mesh.shape[axis] for axis in ("gx", "gy", "gz"))
    return jax.shard_map(
        functools.partial(on_device, *sizes),
        mesh=mesh,
        in_specs=placed,
        out_specs=P(None, "gx", "gy", "gz", None, None),
        check_vma=False,
    )
```

time: 269 us -> 155 us (0.58); the launches traced: 266 us -> 155 us
  Pallas kernels: 0 us -> 151 us
  blocking collectives: 142 us -> 0 us
  waiting for transfers between devices: 52.2 us -> 0 us
  local copies, waits for them, and re-layouts: 31.3 us -> 4.01 us
  matrix products: 19.5 us -> 0 us
  starting transfers between devices: 17 us -> 0 us
  other arithmetic: 3.57 us -> 0 us
    pallas_call x0 -> x1, Pallas kernels: none -> 151 us  [on_device(): pl.pallas_call(functools.partial(kernel, nx, ny, nz, slabs), out_shape=ja...]
    all_to_all x3 -> x0, blocking collectives: 142 us -> none  [the longest x2 94.1 us: on_device(): lax.all_to_all(updated, ('gy', 'gz'), split_axis=1, concat_axis=1, tiled=...]
    all_to_all x1 -> x0, waiting for transfers between devices: 40.4 us -> none  [on_device(): lax.all_to_all(blocks, ('gy', 'gz'), split_axis=1, concat_axis=1, tiled=T...]
    dot_general x11 -> x0, matrix products: 19.5 us -> none  [the longest x2 4.63 us: on_device(): jnp.dot(incoming[1], operators[1], preferred_element_type=jnp.float32)]
    all_to_all x1 -> x0, starting transfers between devices: 13.3 us -> none  [on_device(): lax.all_to_all(blocks, ('gy', 'gz'), split_axis=1, concat_axis=1, tiled=T...]
    reshape x6 -> x1, local copies, waits for them, and re-layouts: 13.3 us -> 1.36 us  [on_device(): face_owner.reshape(plane, 1)]
    ppermute x4 -> x0, waiting for transfers between devices: 11.8 us -> none  [the longest x2 11.2 us: with_halo(): lax.ppermute(lax.slice_in_dim(block, block.shape[dim] - width, None, axis...]
    another operation x6 -> x0, local copies, waits for them, and re-layouts: 9.22 us -> none
  transfers between devices with their start and end apart: 5 -> 0, of which waited for: 4 -> 0; matrix products, arithmetic and copies ran while one was open for 0% -> 0% of each run, Pallas kernels for 0% -> 0%
where the time goes in v1:
time: 155 us
  Pallas kernels  151 us (97%)
  local copies, waits for them, and re-layouts  4.01 us (3%)
    pallas_call x1, Pallas kernels, on_device(): pl.pallas_call(functools.partial(kernel, nx, ny, nz, slabs), out_shape=ja...  151 us

profile of v1, /device:TPU:34, one launch (start us, length us, event | category | flops | bytes accessed | tf_op | source)
XLA Modules:
  0.0 155.3 jit_solution(7415688616119185858)
XLA Ops:
  0.0 1.4 copy.6.owners
  1.4 151.3 %shard_map.55 = bf16[2,512,768]{2,1,0:T(8,128)(2,1)} custom-call(bf16[2,512,768]{2,1,0:T(8,128)(2,1)} %bitcast.10, bf16[2,512,768]{2,1,0:T(8,128)(2,1)} %bitcast.11, bf16[2,768,768]{2,1,0:T(8,128)(2,1)} %bitcast.9, bf16[64,64]{1,0:T(8,128)(2,1)} %bitcast.12, s32[64,1]{1,0:T(8,128)} %copy.6.owners), custom_call_target="tpu_custom_call" | custom-call | tf_op jit(solution)/shard_map/pallas_call | solution.py:301
  152.6 2.7 %copy.9 = bf16[2,1,1,1,512,768]{5,4,3,2,1,0:T(8,128)(2,1)} copy(bf16[2,1,1,1,512,768]{5,4,3,2,1,0:T(8,128)(2,1)} %bitcast.8) | data formatting | bytes 3145728

commit v2 on v1

--- a/solution.py
+++ b/solution.py
@@ -19,9 +19,9 @@
 
 def kernel(
     nx, ny, nz, slabs,
-    traces, sources, ops, coupling, owners, out,
-    in0, in1, in2, sent, xr, zr, kr, ur, zs, sv, bv, mi,
-    load_sem, out_sem, xs_sem, xr_sem, s_sem, r_sem,
+    traces, sources, ops, coupling_hbm, owners_hbm, out,
+    in0, in1, sent, xr, zr, kr, ur, zs, sv, bv, mi, coupling, owners,
+    load_sem, xs_sem, xr_sem, s_sem, r_sem,
 ):
     i = lax.axis_index("gx")
     j = lax.axis_index("gy")
@@ -29,7 +29,7 @@
     rows = 2 * slabs
     block = rows // ny
     plane = ny * nz
-    incoming = (in0, in1, in2)
+    incoming = (in0, in1)
 
     for c in range(2):
         for f in range(FACES):
@@ -38,10 +38,23 @@
                 in0.at[f, pl.ds(c * slabs, slabs), :],
                 load_sem.at[0],
             ).start()
-    load_ops = pltpu.make_async_copy(ops, sv, load_sem.at[1])
-    load_ops.start()
-    load_sources = pltpu.make_async_copy(sources, bv, load_sem.at[2])
-    load_sources.start()
+    tables = [
+        pltpu.make_async_copy(coupling_hbm, coupling, load_sem.at[7]),
+        pltpu.make_async_copy(owners_hbm, owners, load_sem.at[8]),
+    ]
+    loads = []
+    for n, columns in enumerate((pl.ds(2 * W, W), pl.ds(0, 2 * W), pl.ds(3 * W, 3 * W))):
+        load = [
+            pltpu.make_async_copy(ops.at[:, :, columns], sv.at[:, :, columns], load_sem.at[1 + 2 * n]),
+            pltpu.make_async_copy(
+                sources.at[:, :, columns], bv.at[:, :, columns], load_sem.at[2 + 2 * n]
+            ),
+        ]
+        for copy in load:
+            copy.start()
+        loads.append(load)
+    for copy in tables:
+        copy.start()
 
     barrier = pltpu.get_barrier_semaphore()
     left = lax.rem(i + nx - 1, nx)
@@ -165,14 +178,19 @@
         ).start()
 
     def z_return(s, g):
-        mine = pl.ds(pl.multiple_of(j * block, block), block)
-        target = incoming[s + 1]
+        if s == SWEEPS - 1:
+            part = slabs // block
+            rows_at = pl.multiple_of(lax.rem(j, part) * block, block)
+            home = out.at[j // part, pl.ds(rows_at, block), g * W:(g + 1) * W]
+        else:
+            rows_at = pl.multiple_of(j * block, block)
+            home = incoming[s + 1].at[g, pl.ds(rows_at, block), :]
 
         def one(d):
             to = lax.rem(j + d, ny)
             pltpu.make_async_remote_copy(
                 src_ref=zs.at[s, g, to],
-                dst_ref=target.at[g, mine, :],
+                dst_ref=home,
                 send_sem=s_sem.at[s, 3, g],
                 recv_sem=r_sem.at[s, 3, g],
                 device_id={"gy": to},
@@ -181,7 +199,7 @@
 
         ring(ny, one)
         pltpu.make_async_copy(
-            zs.at[s, g, j], target.at[g, mine, :], r_sem.at[s, 3, g]
+            zs.at[s, g, j], home, r_sem.at[s, 3, g]
         ).start()
 
     def arrive(sem, ref):
@@ -199,8 +217,10 @@
 
     def build_mixing():
         owner = jnp.broadcast_to(owners[...], (plane, plane))
-        pick = (owner == lax.broadcasted_iota(jnp.int32, (plane, plane), 1)).astype(jnp.bfloat16)
-        mixing = jnp.dot(coupling[...], pick, preferred_element_type=jnp.float32)
+        pick = (owner == lax.broadcasted_iota(jnp.int32, (plane, plane), 0)).astype(jnp.bfloat16)
+        mixing = lax.dot_general(
+            coupling[...], pick, (((1,), (1,)), ((), ())), preferred_element_type=jnp.float32
+        )
         mixing = mixing.astype(jnp.bfloat16)
 
         def place(index):
@@ -232,13 +252,16 @@
         lax.fori_loop(0, rows // step, part, 0)
 
     arrive(load_sem.at[0], in0)
-    load_ops.wait()
-    load_sources.wait()
+    for copy in loads[0]:
+        copy.wait()
     pl.semaphore_wait(barrier, 2 + (ny - 1) + (nz - 1))
 
     for s in range(SWEEPS):
         local_solve(s, 2)
         z_send(s, 3, sent.at[s, 2])
+        if s == 0:
+            for copy in loads[1] + loads[2] + tables:
+                copy.wait()
         local_solve(s, 0)
         x_send(s, 0, left, 1)
         local_solve(s, 1)
@@ -265,16 +288,8 @@
                 g = ORDER[t - 2]
                 arrive(r_sem.at[s, 2, g], zs.at[s, g])
                 z_return(s, g)
-        target = incoming[s + 1]
         for g in ORDER:
-            arrive(r_sem.at[s, 3, g], target.at[g])
-            if s == SWEEPS - 1:
-                for c in range(2):
-                    pltpu.make_async_copy(
-                        target.at[g, pl.ds(c * slabs, slabs), :],
-                        out.at[c, :, pl.ds(g * W, W)],
-                        out_sem.at[g],
-                    ).start()
+            arrive(r_sem.at[s, 3, g], in0.at[g])
 
     for s in range(SWEEPS):
         for g in range(FACES):
@@ -284,8 +299,6 @@
             arrive(s_sem.at[s, 3, g], zr.at[s, g, pl.ds(0, ny - 1)])
         for slot in range(2):
             arrive(xs_sem.at[s, slot], xr.at[s, slot])
-    for g in range(FACES):
-        arrive(out_sem.at[g], in2.at[g])
 
 
 def on_device(nx, ny, nz, traces, sources, local_ops, plane_coupling, face_owner):
@@ -295,16 +308,15 @@
     plane = ny * nz
     block = rows // ny
     bf16 = jnp.bfloat16
-    hbm = pl.BlockSpec(memory_space=pl.ANY)
+    hbm = pl.BlockSpec(memory_space=pltpu.HBM)
     vmem = pl.BlockSpec(memory_space=pltpu.VMEM)
     faces = (FACES, rows, W)
     out = pl.pallas_call(
         functools.partial(kernel, nx, ny, nz, slabs),
         out_shape=jax.ShapeDtypeStruct((2, slabs, columns), bf16),
-        in_specs=[hbm, hbm, hbm, vmem, vmem],
-        out_specs=hbm,
+        in_specs=[hbm] * 5,
+        out_specs=vmem,
         scratch_shapes=[
-            pltpu.VMEM(faces, bf16),
             pltpu.VMEM(faces, bf16),
             pltpu.VMEM(faces, bf16),
             pltpu.VMEM((SWEEPS,) + faces, bf16),
@@ -316,22 +328,23 @@
             pltpu.VMEM((2, columns, columns), bf16),
             pltpu.VMEM((2, slabs, columns), bf16),
             pltpu.VMEM((rows, rows), bf16),
-            pltpu.SemaphoreType.DMA((3,)),
-            pltpu.SemaphoreType.DMA((FACES,)),
+            pltpu.VMEM((plane, plane), bf16),
+            pltpu.VMEM((1, plane), jnp.int32),
+            pltpu.SemaphoreType.DMA((9,)),
             pltpu.SemaphoreType.DMA((SWEEPS, 2)),
             pltpu.SemaphoreType.DMA((SWEEPS, 2)),
             pltpu.SemaphoreType.DMA((SWEEPS, 4, FACES)),
             pltpu.SemaphoreType.DMA((SWEEPS, 4, FACES)),
         ],
         compiler_params=pltpu.CompilerParams(
-            collective_id=0, has_side_effects=True, vmem_limit_bytes=60 << 20
+            collective_id=0, has_side_effects=True, vmem_limit_bytes=36 << 20
         ),
     )(
-        traces.reshape(2, slabs, columns),
-        sources.reshape(2, slabs, columns),
-        local_ops.reshape(2, columns, columns),
-        plane_coupling.reshape(plane, plane),
-        face_owner.reshape(plane, 1),
+        pltpu.with_memory_space_constraint(traces.reshape(2, slabs, columns), pltpu.HBM),
+        pltpu.with_memory_space_constraint(sources.reshape(2, slabs, columns), pltpu.HBM),
+        pltpu.with_memory_space_constraint(local_ops.reshape(2, columns, columns), pltpu.HBM),
+        pltpu.with_memory_space_constraint(plane_coupling.reshape(plane, plane), pltpu.HBM),
+        pltpu.with_memory_space_constraint(face_owner.reshape(1, plane), pltpu.HBM),
     )
     return out.reshape(traces.shape)
 

time: 155 us -> 151 us (0.974)
  local copies, waits for them, and re-layouts: 4.01 us -> 1.15 us
where the time goes in v2:
time: 151 us
  Pallas kernels  150 us (99%)
    pallas_call x1, Pallas kernels, on_device(): pl.pallas_call(functools.partial(kernel, nx, ny, nz, slabs), out_shape=ja...  150 us

profile of v2, /device:TPU:34, one launch (start us, length us, event | category | flops | bytes accessed | tf_op | source)
XLA Modules:
  0.0 151.2 jit_solution(8118523276934316218)
XLA Ops:
  0.0 150.0 %shard_map.55 = bf16[2,512,768]{2,1,0:T(8,128)(2,1)S(1)} custom-call(bf16[2,512,768]{2,1,0:T(8,128)(2,1)} %bitcast.9, bf16[2,512,768]{2,1,0:T(8,128)(2,1)} %bitcast.10, bf16[2,768,768]{2,1,0:T(8,128)(2,1)} %bitcast.8, bf16[64,64]{1,0:T(8,128)(2,1)} %bitcast.11, s32[1,64]{1,0:T(1,128)} %owners_hbm.1), custom_call_target="tpu_custom_call" | custom-call | tf_op jit(solution)/shard_map/pallas_call | solution.py:314
  150.0 1.1 copy.8

commit v3 on v2

--- a/solution.py
+++ b/solution.py
@@ -90,8 +90,10 @@
 
         lax.fori_loop(0, slabs // step, part, 0)
 
-    def ring(n, body):
+    def ring(n, body, far_first=False):
         def step(t, carry):
+            if far_first:
+                t = n - t
             half = (t + 1) // 2
             odd = lax.rem(t, 2)
             body(odd * half + (1 - odd) * (n - half))
@@ -197,7 +199,7 @@
                 device_id_type=MESH,
             ).start()
 
-        ring(ny, one)
+        ring(ny, one, far_first=True)
         pltpu.make_async_copy(
             zs.at[s, g, j], home, r_sem.at[s, 3, g]
         ).start()
@@ -254,10 +256,10 @@
     arrive(load_sem.at[0], in0)
     for copy in loads[0]:
         copy.wait()
-    pl.semaphore_wait(barrier, 2 + (ny - 1) + (nz - 1))
-
     for s in range(SWEEPS):
         local_solve(s, 2)
+        if s == 0:
+            pl.semaphore_wait(barrier, 2 + (ny - 1) + (nz - 1))
         z_send(s, 3, sent.at[s, 2])
         if s == 0:
             for copy in loads[1] + loads[2] + tables:

time: 151 us -> 150 us (level); the launches traced: 151 us -> 149 us
  Pallas kernels: 150 us -> 147 us
    pallas_call x1, Pallas kernels: 150 us -> 147 us  [on_device(): pl.pallas_call(functools.partial(kernel, nx, ny, nz, slabs), out_shape=ja...]
where the time goes in v3:
time: 150 us; the launch traced here: 149 us
  Pallas kernels  147 us (98%)
    pallas_call x1, Pallas kernels, on_device(): pl.pallas_call(functools.partial(kernel, nx, ny, nz, slabs), out_shape=ja...  147 us

profile of v3, /device:TPU:34, one launch (start us, length us, event | category | flops | bytes accessed | tf_op | source)
XLA Modules:
  0.0 148.6 jit_solution(18108058411292671972)
XLA Ops:
  0.0 147.5 %shard_map.55 = bf16[2,512,768]{2,1,0:T(8,128)(2,1)S(1)} custom-call(bf16[2,512,768]{2,1,0:T(8,128)(2,1)} %bitcast.9, bf16[2,512,768]{2,1,0:T(8,128)(2,1)} %bitcast.10, bf16[2,768,768]{2,1,0:T(8,128)(2,1)} %bitcast.8, bf16[64,64]{1,0:T(8,128)(2,1)} %bitcast.11, s32[1,64]{1,0:T(1,128)} %owners_hbm.1), custom_call_target="tpu_custom_call" | custom-call | tf_op jit(solution)/shard_map/pallas_call | solution.py:316
  147.5 1.1 copy.8

commit v4 on v3

--- a/solution.py
+++ b/solution.py
@@ -12,6 +12,7 @@
 W = 128
 SUB = 16
 ORDER = (3, 2, 5, 4, 0, 1)
+KORDER = (4, 1, 5, 3, 7, 2, 6)
 SHIFT_Y = {2: 1, 3: -1}
 SHIFT_Z = {4: 1, 5: -1}
 MESH = pl.DeviceIdType.MESH
@@ -136,7 +137,8 @@
                 device_id_type=MESH,
             ).start()
 
-        ring(nz, one)
+        for d in KORDER if nz == 8 else range(1, nz):
+            one(d)
         pltpu.make_async_copy(
             zr.at[s, g, :, pl.ds(pl.multiple_of(k * SUB, SUB), SUB), :],
             kr.at[s, g, slot],
@@ -174,7 +176,8 @@
                 device_id_type=MESH,
             ).start()
 
-        ring(nz, one)
+        for d in KORDER if nz == 8 else range(1, nz):
+            one(d)
         pltpu.make_async_copy(
             ur.at[s, g, k], zs.at[s, g, :, mine, :], r_sem.at[s, 2, g]
         ).start()

time: 150 us -> 150 us (level)
  no operation moved by 1% of the time
where the time goes in v4:
time: 150 us; the launch traced here: 148 us
  Pallas kernels  147 us (98%)
    pallas_call x1, Pallas kernels, on_device(): pl.pallas_call(functools.partial(kernel, nx, ny, nz, slabs), out_shape=ja...  147 us

profile of v4, /device:TPU:34, one launch (start us, length us, event | category | flops | bytes accessed | tf_op | source)
XLA Modules:
  0.0 148.5 jit_solution(16367679856192400275)
XLA Ops:
  0.0 147.3 %shard_map.55 = bf16[2,512,768]{2,1,0:T(8,128)(2,1)S(1)} custom-call(bf16[2,512,768]{2,1,0:T(8,128)(2,1)} %bitcast.9, bf16[2,512,768]{2,1,0:T(8,128)(2,1)} %bitcast.10, bf16[2,768,768]{2,1,0:T(8,128)(2,1)} %bitcast.8, bf16[64,64]{1,0:T(8,128)(2,1)} %bitcast.11, s32[1,64]{1,0:T(1,128)} %owners_hbm.1), custom_call_target="tpu_custom_call" | custom-call | tf_op jit(solution)/shard_map/pallas_call | solution.py:319
  147.3 1.1 copy.8
